TPU v7x, 32 devices: a whole 2x2x4 slice. The times are simulated.
32 devices in a mesh: seq: 4 (over y, x), ctx: 8 (over z, core).
Axes of the slice: x: 2, y: 2, z: 4, core: 2. Of those that a mesh axis runs over, the one named last changes fastest.
Arguments:
- hidden_in: bfloat16 [16, 1024, 768], P('seq', 'ctx'), may hold values from -6 to 6
- cotangent: bfloat16 [16, 1024, 768], P('seq', 'ctx'), may hold values from -6 to 6
- segments: int32 [16, 1024], P('seq', 'ctx'), may hold values from 0 to 3, never falling along the last dimension, each value on 1 to 512 neighbouring positions
- qkv_weight: bfloat16 [768, 2304], P('seq'), may hold values from -0.21875 to 0.21875
- query_bias: bfloat16 [768], P('seq'), may hold values from -3 to 3
- value_bias: bfloat16 [768], P('seq'), may hold values from -0.29882812 to 0.29882812
- out_weight: bfloat16 [768, 768], P('seq'), may hold values from -1.75 to 1.75
- out_bias: bfloat16 [768], P('seq'), may hold values from -2 to 2
- first_gain: bfloat16 [768], P('seq'), may hold values from 0.5 to 1.5
- first_shift: bfloat16 [768], P('seq'), may hold values from -2 to 2
- inner_weight: bfloat16 [768, 3072], P('seq'), may hold values from -0.21875 to 0.21875
- inner_bias: bfloat16 [3072], P('seq'), may hold values from -3 to 3
- outer_weight: bfloat16 [3072, 768], P('seq'), may hold values from -0.21875 to 0.21875
- outer_bias: bfloat16 [768], P('seq'), may hold values from -2 to 2
- second_gain: bfloat16 [768], P('seq'), may hold values from 0.5 to 1.5
- second_shift: bfloat16 [768], P('seq'), may hold values from -2 to 2
Outputs:
- output: bfloat16 [16, 1024, 768], P('seq', 'ctx')
- grad_input: float32 [16, 1024, 768], P('seq', 'ctx')
- grad_qkv_weight: float32 [768, 2304], P('seq')
- grad_query_bias: float32 [768], P('seq')
- grad_value_bias: float32 [768], P('seq')
- grad_out_weight: float32 [768, 768], P('seq')
- grad_out_bias: float32 [768], P('seq')
- grad_first_gain: float32 [768], P('seq')
- grad_first_shift: float32 [768], P('seq')
- grad_inner_weight: float32 [768, 3072], P('seq')
- grad_inner_bias: float32 [3072], P('seq')
- grad_outer_weight: float32 [3072, 768], P('seq')
- grad_outer_bias: float32 [768], P('seq')
- grad_second_gain: float32 [768], P('seq')
- grad_second_shift: float32 [768], P('seq')
Inputs may be any that keep to these rules, and one draw needn't show every extreme that they name: `segments`: in each sequence the document numbers never fall along the positions; a document holds 1 to 512 positions, and some document holds exactly 512; attention joins only positions of one document of one sequence.
All inputs are finite; a program needn't handle non-finite values.
Results may differ from a plain program's by a relative error of at most 0.035.
Values may be sent and summed in bfloat16 or wider, within the bound.
A program may use at most 320 MiB of HBM per device.

v0:
```python
from functools import partial
import jax
import jax.numpy as jnp
from jax import lax
from jax.sharding import PartitionSpec as P

HEADS = 12
HEAD_DIM = 64
norm_epsilon = 1e-12


def norm_forward(matrix, gain, shift):
    average = jnp.mean(matrix, axis=-1, keepdims=True)
    centred = matrix - average
    factor = lax.rsqrt(jnp.mean(centred * centred, axis=-1, keepdims=True) + norm_epsilon)
    normed = centred * factor
    return (normed * gain + shift, normed, factor)


def norm_backward(upstream, normed, factor, gain):
    scaled = upstream * gain
    return factor * (
        scaled
        - jnp.mean(scaled, axis=-1, keepdims=True)
        - normed * jnp.mean(scaled * normed, axis=-1, keepdims=True)
    )


def split_heads(matrix):
    groups, positions, widths = matrix.shape
    return jnp.moveaxis(matrix.reshape(groups, positions, HEADS, widths // HEADS), 2, 0)


def join_heads(matrix):
    return jnp.moveaxis(matrix, 0, 2).reshape(
        matrix.shape[1], matrix.shape[2], matrix.shape[0] * matrix.shape[3]
    )


def grads_block(query_one, upstream_one, lse_one, delta_one, key_one, value_one, allowed, scaling):
    scores = (
        jnp.einsum("sqd,skd->sqk", query_one, key_one, preferred_element_type=jnp.float32) * scaling
    )
    probability = jnp.exp(jnp.where(allowed, scores - lse_one[..., None], -1e30))
    grad_probs = jnp.einsum(
        "sqd,skd->sqk", upstream_one, value_one, preferred_element_type=jnp.float32
    )
    grad_scores = (probability * (grad_probs - delta_one[..., None])).astype(jnp.bfloat16)
    grad_query = (
        jnp.einsum("sqk,skd->sqd", grad_scores, key_one, preferred_element_type=jnp.float32)
        * scaling
    )
    grad_key = (
        jnp.einsum("sqk,sqd->skd", grad_scores, query_one, preferred_element_type=jnp.float32)
        * scaling
    )
    grad_value = jnp.einsum(
        "sqk,sqd->skd",
        probability.astype(jnp.bfloat16),
        upstream_one,
        preferred_element_type=jnp.float32,
    )
    return (grad_query, grad_key, grad_value)


def on_device(
    hidden_in,
    cotangent,
    segments,
    qkv_weight,
    query_bias,
    value_bias,
    out_weight,
    out_bias,
    first_gain,
    first_shift,
    inner_weight,
    inner_bias,
    outer_weight,
    outer_bias,
    second_gain,
    second_shift,
):
    groups, positions, model_width = hidden_in.shape
    row_count = groups * positions
    scaling = HEAD_DIM ** (-0.5)
    gathered = (
        lax.all_gather(qkv_weight, "seq", axis=0, tiled=True),
        lax.all_gather(query_bias, "seq", axis=0, tiled=True),
        lax.all_gather(value_bias, "seq", axis=0, tiled=True),
        lax.all_gather(out_weight, "seq", axis=0, tiled=True),
        lax.all_gather(out_bias, "seq", axis=0, tiled=True),
        lax.all_gather(first_gain, "seq", axis=0, tiled=True),
        lax.all_gather(first_shift, "seq", axis=0, tiled=True),
        lax.all_gather(inner_weight, "seq", axis=0, tiled=True),
        lax.all_gather(inner_bias, "seq", axis=0, tiled=True),
        lax.all_gather(outer_weight, "seq", axis=0, tiled=True),
        lax.all_gather(outer_bias, "seq", axis=0, tiled=True),
        lax.all_gather(second_gain, "seq", axis=0, tiled=True),
        lax.all_gather(second_shift, "seq", axis=0, tiled=True),
    )
    (
        qkv_full,
        qbias_full,
        vbias_full,
        out_full,
        obias_full,
        fgain_full,
        fshift_full,
        inner_full,
        ibias_full,
        outer_full,
        ubias_full,
        sgain_full,
        sshift_full,
    ) = gathered
    token_rows = hidden_in.reshape(row_count, model_width)
    projected = jnp.dot(token_rows, qkv_full, preferred_element_type=jnp.float32)
    queries_low = (
        (projected[:, :model_width] + qbias_full)
        .astype(jnp.bfloat16)
        .reshape(groups, positions, model_width)
    )
    keys_low = (
        projected[:, model_width : 2 * model_width]
        .astype(jnp.bfloat16)
        .reshape(groups, positions, model_width)
    )
    values_low = (
        (projected[:, 2 * model_width :] + vbias_full)
        .astype(jnp.bfloat16)
        .reshape(groups, positions, model_width)
    )
    seg_low = segments.astype(jnp.bfloat16)
    query_heads = split_heads(queries_low)
    start_state = (
        jnp.full((HEADS, groups, positions), -1e30, jnp.float32),
        jnp.zeros((HEADS, groups, positions), jnp.float32),
        jnp.zeros((HEADS, groups, positions, HEAD_DIM), jnp.float32),
    )
    key_part = lax.all_gather(keys_low, "ctx", axis=1, tiled=True)
    value_part = lax.all_gather(values_low, "ctx", axis=1, tiled=True)
    seg_part = lax.all_gather(seg_low, "ctx", axis=1, tiled=True)
    fold_allowed = seg_low[:, :, None] == seg_part[:, None, :]

    def per_head(head_item):
        query_one, key_one, value_one, old_max, old_total, old_acc = head_item
        scores = (
            jnp.einsum("sqd,skd->sqk", query_one, key_one, preferred_element_type=jnp.float32)
            * scaling
        )
        scores = jnp.where(fold_allowed, scores, -1e30)
        new_max = jnp.maximum(old_max, jnp.max(scores, axis=-1))
        retain = jnp.exp(old_max - new_max)
        weights = jnp.where(fold_allowed, jnp.exp(scores - new_max[..., None]), 0.0)
        run_total = old_total * retain + jnp.sum(weights, axis=-1)
        run_acc = old_acc * retain[..., None] + jnp.einsum(
            "sqk,skd->sqd",
            weights.astype(jnp.bfloat16),
            value_one,
            preferred_element_type=jnp.float32,
        )
        return (new_max, run_total, run_acc)

    run_max, run_total, run_acc = lax.map(
        per_head,
        (
            query_heads,
            split_heads(key_part),
            split_heads(value_part),
            start_state[0],
            start_state[1],
            start_state[2],
        ),
    )
    out_heads = run_acc / run_total[..., None]
    row_lse = run_max + jnp.log(run_total)
    context_low = join_heads(out_heads).reshape(row_count, model_width).astype(jnp.bfloat16)
    attended = jnp.dot(context_low, out_full, preferred_element_type=jnp.float32) + obias_full
    residual = token_rows.astype(jnp.float32) + attended
    first, first_normed, first_factor = norm_forward(residual, fgain_full, fshift_full)
    first_low = first.astype(jnp.bfloat16)
    inner = jnp.dot(first_low, inner_full, preferred_element_type=jnp.float32) + ibias_full
    active = jax.nn.gelu(inner, approximate=False).astype(jnp.bfloat16)
    branch = jnp.dot(active, outer_full, preferred_element_type=jnp.float32) + ubias_full
    result, second_normed, second_factor = norm_forward(first + branch, sgain_full, sshift_full)
    output = result.astype(jnp.bfloat16).reshape(groups, positions, model_width)
    qkv_back, out_back, inner_back, outer_back, fgain_back, sgain_back = (
        lax.all_gather(qkv_weight, "seq", axis=0, tiled=True),
        lax.all_gather(out_weight, "seq", axis=0, tiled=True),
        lax.all_gather(inner_weight, "seq", axis=0, tiled=True),
        lax.all_gather(outer_weight, "seq", axis=0, tiled=True),
        lax.all_gather(first_gain, "seq", axis=0, tiled=True),
        lax.all_gather(second_gain, "seq", axis=0, tiled=True),
    )
    grad_out = cotangent.reshape(row_count, model_width).astype(jnp.float32)
    grad_second_gain = jnp.sum(grad_out * second_normed, axis=0)
    grad_second_shift = jnp.sum(grad_out, axis=0)
    grad_second = norm_backward(grad_out, second_normed, second_factor, sgain_back)
    grad_branch = grad_second.astype(jnp.bfloat16)
    grad_outer_weight = jnp.einsum(
        "rf,rd->fd", active, grad_branch, preferred_element_type=jnp.float32
    )
    grad_outer_bias = jnp.sum(grad_branch.astype(jnp.float32), axis=0)
    grad_active = jnp.einsum(
        "rd,fd->rf", grad_branch, outer_back, preferred_element_type=jnp.float32
    )
    _, gelu_pull = jax.vjp(partial(jax.nn.gelu, approximate=False), inner)
    grad_inner = gelu_pull(grad_active)[0].astype(jnp.bfloat16)
    grad_inner_weight = jnp.einsum(
        "rd,rf->df", first_low, grad_inner, preferred_element_type=jnp.float32
    )
    grad_inner_bias = jnp.sum(grad_inner.astype(jnp.float32), axis=0)
    grad_first = grad_second + jnp.einsum(
        "rf,df->rd", grad_inner, inner_back, preferred_element_type=jnp.float32
    )
    grad_first_gain = jnp.sum(grad_first * first_normed, axis=0)
    grad_first_shift = jnp.sum(grad_first, axis=0)
    grad_residual = norm_backward(grad_first, first_normed, first_factor, fgain_back)
    grad_attended = grad_residual.astype(jnp.bfloat16)
    grad_out_weight = jnp.einsum(
        "rd,re->de", context_low, grad_attended, preferred_element_type=jnp.float32
    )
    grad_out_bias = jnp.sum(grad_attended.astype(jnp.float32), axis=0)
    grad_context = jnp.einsum(
        "re,de->rd", grad_attended, out_back, preferred_element_type=jnp.float32
    )
    grad_context = grad_context.astype(jnp.bfloat16).reshape(groups, positions, model_width)
    grad_heads = split_heads(grad_context)
    row_delta = jnp.sum(grad_heads.astype(jnp.float32) * out_heads, axis=-1)
    far_keys, far_values, far_segs = (
        lax.all_gather(keys_low, "ctx", axis=1, tiled=True),
        lax.all_gather(values_low, "ctx", axis=1, tiled=True),
        lax.all_gather(seg_low, "ctx", axis=1, tiled=True),
    )
    allowed = seg_low[:, :, None] == far_segs[:, None, :]

    def head_keys(head_item):
        query_one, upstream_one, lse_one, delta_one, key_one, value_one = head_item
        return grads_block(
            query_one, upstream_one, lse_one, delta_one, key_one, value_one, allowed, scaling
        )

    dq_heads, dk_heads, dv_heads = lax.map(
        head_keys,
        (
            query_heads,
            grad_heads,
            row_lse,
            row_delta,
            split_heads(far_keys),
            split_heads(far_values),
        ),
    )
    key_grad, value_grad = (
        lax.psum_scatter(
            join_heads(dk_heads).astype(jnp.bfloat16), "ctx", scatter_dimension=1, tiled=True
        ).astype(jnp.float32),
        lax.psum_scatter(
            join_heads(dv_heads).astype(jnp.bfloat16), "ctx", scatter_dimension=1, tiled=True
        ).astype(jnp.float32),
    )
    query_grad = join_heads(dq_heads)
    query_low_grad = query_grad.reshape(row_count, model_width).astype(jnp.bfloat16)
    key_low_grad = key_grad.reshape(row_count, model_width).astype(jnp.bfloat16)
    value_low_grad = value_grad.reshape(row_count, model_width).astype(jnp.bfloat16)
    grad_projected = jnp.concatenate([query_low_grad, key_low_grad, value_low_grad], axis=1)
    grad_qkv_weight = jnp.einsum(
        "rd,rf->df", token_rows, grad_projected, preferred_element_type=jnp.float32
    )
    grad_query_bias = jnp.sum(query_low_grad.astype(jnp.float32), axis=0)
    grad_value_bias = jnp.sum(value_low_grad.astype(jnp.float32), axis=0)
    grad_input = grad_residual + jnp.einsum(
        "rf,df->rd", grad_projected, qkv_back, preferred_element_type=jnp.float32
    )
    owned = (
        lax.psum_scatter(
            grad_qkv_weight.astype(jnp.bfloat16), "seq", scatter_dimension=0, tiled=True
        ).astype(jnp.float32),
        lax.psum_scatter(
            grad_query_bias.astype(jnp.bfloat16), "seq", scatter_dimension=0, tiled=True
        ).astype(jnp.float32),
        lax.psum_scatter(
            grad_value_bias.astype(jnp.bfloat16), "seq", scatter_dimension=0, tiled=True
        ).astype(jnp.float32),
        lax.psum_scatter(
            grad_out_weight.astype(jnp.bfloat16), "seq", scatter_dimension=0, tiled=True
        ).astype(jnp.float32),
        lax.psum_scatter(
            grad_out_bias.astype(jnp.bfloat16), "seq", scatter_dimension=0, tiled=True
        ).astype(jnp.float32),
        lax.psum_scatter(
            grad_first_gain.astype(jnp.bfloat16), "seq", scatter_dimension=0, tiled=True
        ).astype(jnp.float32),
        lax.psum_scatter(
            grad_first_shift.astype(jnp.bfloat16), "seq", scatter_dimension=0, tiled=True
        ).astype(jnp.float32),
        lax.psum_scatter(
            grad_inner_weight.astype(jnp.bfloat16), "seq", scatter_dimension=0, tiled=True
        ).astype(jnp.float32),
        lax.psum_scatter(
            grad_inner_bias.astype(jnp.bfloat16), "seq", scatter_dimension=0, tiled=True
        ).astype(jnp.float32),
        lax.psum_scatter(
            grad_outer_weight.astype(jnp.bfloat16), "seq", scatter_dimension=0, tiled=True
        ).astype(jnp.float32),
        lax.psum_scatter(
            grad_outer_bias.astype(jnp.bfloat16), "seq", scatter_dimension=0, tiled=True
        ).astype(jnp.float32),
        lax.psum_scatter(
            grad_second_gain.astype(jnp.bfloat16), "seq", scatter_dimension=0, tiled=True
        ).astype(jnp.float32),
        lax.psum_scatter(
            grad_second_shift.astype(jnp.bfloat16), "seq", scatter_dimension=0, tiled=True
        ).astype(jnp.float32),
    )
    summed = (
        lax.psum(owned[0].astype(jnp.bfloat16), "ctx").astype(jnp.float32),
        lax.psum(owned[1].astype(jnp.bfloat16), "ctx").astype(jnp.float32),
        lax.psum(owned[2].astype(jnp.bfloat16), "ctx").astype(jnp.float32),
        lax.psum(owned[3].astype(jnp.bfloat16), "ctx").astype(jnp.float32),
        lax.psum(owned[4].astype(jnp.bfloat16), "ctx").astype(jnp.float32),
        lax.psum(owned[5].astype(jnp.bfloat16), "ctx").astype(jnp.float32),
        lax.psum(owned[6].astype(jnp.bfloat16), "ctx").astype(jnp.float32),
        lax.psum(owned[7].astype(jnp.bfloat16), "ctx").astype(jnp.float32),
        lax.psum(owned[8].astype(jnp.bfloat16), "ctx").astype(jnp.float32),
        lax.psum(owned[9].astype(jnp.bfloat16), "ctx").astype(jnp.float32),
        lax.psum(owned[10].astype(jnp.bfloat16), "ctx").astype(jnp.float32),
        lax.psum(owned[11].astype(jnp.bfloat16), "ctx").astype(jnp.float32),
        lax.psum(owned[12].astype(jnp.bfloat16), "ctx").astype(jnp.float32),
    )
    return (
        output,
        grad_input.reshape(groups, positions, model_width),
        summed[0],
        summed[1],
        summed[2],
        summed[3],
        summed[4],
        summed[5],
        summed[6],
        summed[7],
        summed[8],
        summed[9],
        summed[10],
        summed[11],
        summed[12],
    )


def solution(mesh):
    placed = (
        P("seq", "ctx", None),
        P("seq", "ctx", None),
        P("seq", "ctx"),
        P("seq", None),
        P("seq"),
        P("seq"),
        P("seq", None),
        P("seq"),
        P("seq"),
        P("seq"),
        P("seq", None),
        P("seq"),
        P("seq", None),
        P("seq"),
        P("seq"),
        P("seq"),
    )
    return jax.shard_map(
        on_device,
        mesh=mesh,
        in_specs=placed,
        out_specs=(
            P("seq", "ctx", None),
            P("seq", "ctx", None),
            P("seq", None),
            P("seq"),
            P("seq"),
            P("seq", None),
            P("seq"),
            P("seq"),
            P("seq"),
            P("seq", None),
            P("seq"),
            P("seq", None),
            P("seq"),
            P("seq"),
            P("seq"),
        ),
        check_vma=False,
    )
```

profile of v0, /device:TPU:0, one launch (start us, length us, event | category | flops | bytes accessed | tf_op | source)
XLA Modules:
  0.0 961.4 jit_solution(5188691105644556815)
XLA Ops:
  15.8 17.8 %all-reduce.20 = (bf16[768]{0:T(1024)(128)(2,1)S(1)}, bf16[768]{0:T(1024)(128)(2,1)S(1)}, bf16[768]{0:T(1024)(128)(2,1)S(1)}, bf16[768]{0:T(1024)(128)(2,1)S(1)}...) all-reduce(bf16[768]{0:T(1024)(128)(2,1)S(1)} %dynamic-update-slice, ...), channel_id=1, replica_groups=mesh['seq'=4,'ctx'=8] {'seq'}, use_global_device_ids=true, to_apply=%add | all-reduce | flops 5376 | bytes 21504
  33.7 26.3 %all-gather.8.cloned.1.call-done = bf16[768,2304]{1,0:T(8,128)(2,1)} async-done(((bf16[192,2304]{1,0:T(8,128)(2,1)}), bf16[768,2304]{1,0:T(8,128)(2,1)}) %all-gather.8.cloned.1.call-update) | async-done | bytes 3538960 | tf_op jit(solution)/shard_map/all_gather | solution.py:88
  72.2 11.9 %all_gather.60 = bf16[4,1024]{1,0:T(4,128)(2,1)S(1)} all-gather(bf16[4,128]{1,0:T(4,128)(2,1)S(1)} %convert_element_type.236), channel_id=1, replica_groups=mesh['seq'=4,'ctx'=8] {'ctx'}, dimensions={1}, use_global_device_ids=true | all-gather | bytes 9216 | tf_op jit(solution)/shard_map/all_gather | solution.py:143
  84.1 8.2 all-gather
  96.5 36.3 %all-gather.12.cloned.1.call-done = bf16[4,1024,768]{1,2,0:T(8,128)(2,1)} async-done(((bf16[4,128,768]{1,2,0:T(8,128)(2,1)}), bf16[4,1024,768]{1,2,0:T(8,128)(2,1)}) %all-gather.12.cloned.1.call-update) | async-done | bytes 6291472 | tf_op jit(solution)/shard_map/all_gather | solution.py:142
  132.9 6.7 copy.57
  139.6 58.8 %all-gather.10.cloned.1.call-done = bf16[4,1024,768]{1,2,0:T(8,128)(2,1)} async-done(((bf16[4,128,768]{1,2,0:T(8,128)(2,1)}), bf16[4,1024,768]{1,2,0:T(8,128)(2,1)}) %all-gather.10.cloned.1.call-update) | async-done | bytes 6291472 | tf_op jit(solution)/shard_map/all_gather | solution.py:141
  198.4 6.7 copy.56
  205.1 51.8 %while.30 = (s32[]{:T(128)}, f32[12,4,128]{2,1,0:T(4,128)S(1)}, f32[12,4,128]{2,1,0:T(4,128)S(1)}, f32[12,4,128,64]{2,1,3,0:T(4,128)S(1)}, bf16[12,4,128,64]{2,3...) while((s32[]{:T(128)}, f32[12,4,128]{2,1,0:T(4,128)S(1)}, ...), condition=%wide.region_3.4_spmd.clone, body=%wide.region_0.3_spmd.clone.sunk | while | flops 142641664 | bytes 7852653 | solution.py:165
  261.0 23.9 %all-gather.16.cloned.1.call-done = bf16[768,3072]{1,0:T(8,128)(2,1)} async-done(((bf16[192,3072]{1,0:T(8,128)(2,1)}), bf16[768,3072]{1,0:T(8,128)(2,1)}) %all-gather.16.cloned.1.call-update) | async-done | bytes 4718608 | tf_op jit(solution)/shard_map/all_gather | solution.py:95
  284.9 19.8 %multiply_convert_fusion.1 = (bf16[512,3072]{1,0:T(8,128)(2,1)}, f32[512,3072]{1,0:T(8,128)}, f32[512,3072]{1,0:T(8,128)}) fusion(f32[3072]{0:T(1024)S(1)} %bitcast.237, bf16[768,3072]{1,0:T(8,128)(2,1)} %all-gather.16.cloned.1.call-done, f32[512,768]{1,0:T(8,128)S(1)} %get-tuple-element.358, f32[768]{0:T(1024)S(1)} %convert_element_type.244, ...), kind=kOutput, calls=%fused_computation.66 | convolution fusion | flops 2521694208 | bytes 22042624 | tf_op jit(solution)/shard_map/dot_general | solution.py:183
  304.7 39.0 %all-gather.18.cloned.1.call-done = bf16[3072,768]{1,0:T(8,128)(2,1)} async-done(((bf16[768,768]{1,0:T(8,128)(2,1)}), bf16[3072,768]{1,0:T(8,128)(2,1)}) %all-gather.18.cloned.1.call-update) | async-done | bytes 4718608 | tf_op jit(solution)/shard_map/all_gather | solution.py:97
  343.7 6.5 fusion.84
  353.2 9.2 fusion.85
  375.0 103.3 %while.31 = (s32[]{:T(128)}, bf16[12,4,128,64]{2,3,1,0:T(8,128)(2,1)}, bf16[12,4,1024,64]{2,3,0,1:T(8,128)(2,1)}, bf16[12,4,1024,64]{2,3,0,1:T(8,128)(2,1)}, bf1...) while((s32[]{:T(128)}, ...), condition=%wide.region_14.15_spmd.clone, body=%wide.region_13.14_spmd.clone.sunk | while | flops 340033536 | bytes 13657221 | solution.py:244
  478.3 10.8 %copy.70 = bf16[4,1024,768]{2,0,1:T(4,128)(2,1)} copy(bf16[4,1024,768]{1,2,0:T(8,128)(2,1)} %bitcast.219) | data formatting | bytes 12582912
  489.0 6.9 copy.100
  496.0 11.0 %copy.72 = bf16[4,1024,768]{2,0,1:T(4,128)(2,1)} copy(bf16[4,1024,768]{1,2,0:T(8,128)(2,1)} %bitcast.220) | data formatting | bytes 12582912
  507.0 7.0 copy.102
  516.8 49.2 %reduce-scatter.19.cloned.1.call-done = bf16[128,3072]{1,0:T(8,128)(2,1)} async-done(((bf16[1024,3072]{1,0:T(8,128)(2,1)}), bf16[128,3072]{1,0:T(8,128)(2,1)}) %reduce-scatter.19.cloned.1.call-update) | async-done | bytes 786448
  569.3 67.2 %reduce-scatter.21.cloned.1.call-done = bf16[128,3072]{1,0:T(8,128)(2,1)} async-done(((bf16[1024,3072]{1,0:T(8,128)(2,1)}), bf16[128,3072]{1,0:T(8,128)(2,1)}) %reduce-scatter.21.cloned.1.call-update) | async-done | bytes 786448
  649.5 5.8 copy.74
  659.1 7.9 convolution_convert_fusion.1
  667.2 7.4 convolution_convert_fusion
  674.7 26.5 %reduce-scatter.23.cloned.1.call-done = bf16[192,2304]{1,0:T(8,128)(2,1)} async-done(((bf16[768,2304]{1,0:T(8,128)(2,1)}), bf16[192,2304]{1,0:T(8,128)(2,1)}) %reduce-scatter.23.cloned.1.call-update) | async-done | bytes 884752
  703.5 29.0 %reduce-scatter.13.cloned.1.call-done = bf16[192,768]{1,0:T(8,128)(2,1)} async-done(((bf16[768,768]{1,0:T(8,128)(2,1)}), bf16[192,768]{1,0:T(8,128)(2,1)}) %reduce-scatter.13.cloned.1.call-update) | async-done | bytes 294928 | tf_op jit(solution)/shard_map/reduce_scatter | solution.py:286
  732.5 60.1 %reduce-scatter.15.cloned.1.call-done = bf16[192,3072]{1,0:T(8,128)(2,1)} async-done(((bf16[768,3072]{1,0:T(8,128)(2,1)}), bf16[192,3072]{1,0:T(8,128)(2,1)}) %reduce-scatter.15.cloned.1.call-update) | async-done | bytes 1179664 | tf_op jit(solution)/shard_map/reduce_scatter | solution.py:298
  792.6 60.0 %reduce-scatter.17.cloned.1.call-done = bf16[768,768]{1,0:T(8,128)(2,1)} async-done(((bf16[3072,768]{1,0:T(8,128)(2,1)}), bf16[768,768]{1,0:T(8,128)(2,1)}) %reduce-scatter.17.cloned.1.call-update) | async-done | bytes 1179664 | tf_op jit(solution)/shard_map/reduce_scatter | solution.py:304
  856.1 15.5 %all-reduce.19 = (bf16[768]{0:T(1024)(128)(2,1)S(1)}, bf16[768]{0:T(1024)(128)(2,1)S(1)}, bf16[768]{0:T(1024)(128)(2,1)S(1)}, bf16[768]{0:T(1024)(128)(2,1)S(1)}...) all-reduce(bf16[768]{0:T(1024)(128)(2,1)S(1)} %dynamic-update-slice, ...), channel_id=1, replica_groups=mesh['seq'=4,'ctx'=8] {'seq'}, use_global_device_ids=true, to_apply=%add.7 | all-reduce | flops 9984 | bytes 39936
  872.3 15.2 %all-reduce.17 = (bf16[192]{0:T(256)(128)(2,1)S(1)}, bf16[192]{0:T(256)(128)(2,1)S(1)}, bf16[192]{0:T(256)(128)(2,1)S(1)}, bf16[192]{0:T(256)(128)(2,1)S(1)}, bf...) all-reduce(bf16[192]{0:T(256)(128)(2,1)S(1)} %dynamic-slice.9, ...), channel_id=1, replica_groups=mesh['seq'=4,'ctx'=8] {'ctx'}, use_global_device_ids=true, to_apply=%region_21.22 | all-reduce | flops 2304 | bytes 9216 | tf_op jit(solution)/shard_map/psum | solution.py:319
  893.8 5.9 convolution_add_fusion.1
  899.7 47.9 %all-reduce.23.cloned.1.call-done = (bf16[192,2304]{0,1:T(8,128)(2,1)}, bf16[192,768]{1,0:T(8,128)(2,1)}, bf16[192,3072]{1,0:T(8,128)(2,1)}, bf16[768,768]{1,0:T(8,128)(2,1)}) async-done(((bf16[192,2304]{0,1:T(8,128)(2,1)}, bf16[192,768]{1,0:T(8,128)(2,1)}, bf16[192,3072]{1,0:T(8,128)(2,1)}, bf16[768,768]{1,0:T(8,128)(2,1)}), (bf16[192,2304]{0,1:T(8,128)(2,1)}, bf16[192,768]{1,0:T(8,128)(2,1)}, ...) | async-done | bytes 3538960 | tf_op jit(solution)/shard_map/psum | solution.py:318
  (325 shorter events, 239.6 us)
Async XLA Ops:
  7.2 52.8 %all-gather.8.cloned.1.call-start = ((), (), s32[]{:S(2)}) async-start(), calls=%async_computation.6 | async-start | bytes 4423680 | tf_op jit(solution)/shard_map/all_gather | solution.py:88
  7.9 125.0 %all-gather.12.cloned.1.call-start = ((), (), s32[]{:S(2)}) async-start(), calls=%async_computation.8 | async-start | bytes 7077888 | tf_op jit(solution)/shard_map/all_gather | solution.py:142
  64.2 2.1 copy-start.6
  67.5 130.9 %all-gather.10.cloned.1.call-start = ((), (), s32[]{:S(2)}) async-start(), calls=%async_computation.7 | async-start | bytes 7077888 | tf_op jit(solution)/shard_map/all_gather | solution.py:141
  69.1 3.1 copy-start.12
  69.1 15.0 %copy-start.13 = (bf16[768]{0:T(1024)(128)(2,1)S(1)}, bf16[768]{0:T(1024)(128)(2,1)}, u32[]{:S(2)}) copy-start(bf16[768]{0:T(1024)(128)(2,1)} %param.31) | copy-start | bytes 4612
  69.1 23.2 %copy-start = (bf16[4,128,768]{2,1,0:T(8,128)(2,1)S(1)}, bf16[4,128,768]{2,1,0:T(8,128)(2,1)}, u32[]{:S(2)}) copy-start(bf16[4,128,768]{2,1,0:T(8,128)(2,1)} %param.21) | copy-start | bytes 2359300
  70.3 187.0 %all-gather.14.cloned.1.call-start = ((), (), s32[]{:S(2)}) async-start(), calls=%async_computation.9 | async-start | bytes 1474560 | tf_op jit(solution)/shard_map/all_gather | solution.py:91
  70.9 214.0 %all-gather.16.cloned.1.call-start = ((), (), s32[]{:S(2)}) async-start(), calls=%async_computation.10 | async-start | bytes 5898240 | tf_op jit(solution)/shard_map/all_gather | solution.py:95
  71.5 272.2 %all-gather.18.cloned.1.call-start = ((), (), s32[]{:S(2)}) async-start(), calls=%async_computation.11 | async-start | bytes 5898240 | tf_op jit(solution)/shard_map/all_gather | solution.py:97
  72.0 493.9 %reduce-scatter.19.cloned.1.call-start = ((), (), s32[]{:S(2)}) async-start(), calls=%async_computation.15 | async-start | bytes 7077888
  256.9 1.1 copy-start.5
  257.2 3.4 copy-start.7
  260.7 44.0 %copy-start.3 = (f32[512,768]{1,0:T(8,128)}, f32[512,768]{1,0:T(8,128)S(1)}, u32[]{:S(2)}) copy-start(f32[512,768]{1,0:T(8,128)S(1)} %get-tuple-element.358) | copy-start | bytes 4718596
  350.5 2.8 copy-start.14
  351.1 11.3 %slice-start = ((s8[4718592]{0:T(1024)(128)(4,1)}), s8[4194304]{0:T(1024)(128)(4,1)S(1)}, s32[]{:S(2)}) async-start(s8[4718592]{0:T(1024)(128)(4,1)} %bitcast.239), calls=%async_computation.19 | async-start | bytes 8388608
  351.7 10.7 %copy-start.8 = (f32[512,768]{1,0:T(8,128)}, f32[512,768]{1,0:T(8,128)S(1)}, u32[]{:S(2)}) copy-start(f32[512,768]{1,0:T(8,128)S(1)} %get-tuple-element.340) | copy-start | bytes 4718596
  353.2 9.2 copy-start.4
  353.2 9.2 slice-start.1
  367.6 1.7 copy-start.15
  496.0 140.5 %reduce-scatter.21.cloned.1.call-start = ((), (), s32[]{:S(2)}) async-start(), calls=%async_computation.16 | async-start | bytes 7077888
  514.0 187.1 %reduce-scatter.23.cloned.1.call-start = ((), (), s32[]{:S(2)}) async-start(), calls=%async_computation.17 | async-start | bytes 4423680
  639.8 4.3 copy-start.16
  655.4 77.1 %reduce-scatter.13.cloned.1.call-start = ((), (), s32[]{:S(2)}) async-start(), calls=%async_computation.12 | async-start | bytes 1474560 | tf_op jit(solution)/shard_map/reduce_scatter | solution.py:286
  658.9 133.7 %reduce-scatter.15.cloned.1.call-start = ((), (), s32[]{:S(2)}) async-start(), calls=%async_computation.13 | async-start | bytes 5898240 | tf_op jit(solution)/shard_map/reduce_scatter | solution.py:298
  667.1 185.5 %reduce-scatter.17.cloned.1.call-start = ((), (), s32[]{:S(2)}) async-start(), calls=%async_computation.14 | async-start | bytes 5898240 | tf_op jit(solution)/shard_map/reduce_scatter | solution.py:304
  674.6 273.0 %all-reduce.23.cloned.1.call-start = ((), (), s32[]{:S(2)}) async-start(), calls=%async_computation.18 | async-start | bytes 7667712 | tf_op jit(solution)/shard_map/psum | solution.py:318
  703.4 150.6 %copy-start.17 = (bf16[192]{0:T(256)(128)(2,1)S(1)}, bf16[192]{0:T(256)(128)(2,1)}, u32[]{:S(2)}) copy-start(bf16[192]{0:T(256)(128)(2,1)} %param.35) | copy-start | bytes 1156
  856.1 37.7 %copy-start.2 = (f32[512,768]{1,0:T(8,128)S(1)}, f32[512,768]{1,0:T(8,128)}, u32[]{:S(2)}) copy-start(f32[512,768]{1,0:T(8,128)} %copy-done.1) | copy-start | bytes 4718596
  947.6 3.0 copy-start.9
  950.7 1.7 copy-start.10
  952.3 1.6 copy-start.11
  (1 other events, 1.1 us)
Sparse Core Ops, SparseCore 0:
  9.9 50.0 all-gather.7
  67.7 65.1 all-gather.11
  135.0 63.2 all-gather.9
  200.1 25.9 all-gather.13
  227.7 57.1 all-gather.15
  286.6 57.0 all-gather.17
  496.1 69.7 reduce-scatter.18
  568.2 68.1 reduce-scatter.20
  655.5 45.5 reduce-scatter.22
  703.9 28.5 reduce-scatter.12
  735.5 57.0 reduce-scatter.14
  795.4 57.0 reduce-scatter.16
  855.8 91.8 all-reduce.22
where the time goes:
time: 970 us; the launch traced here: 961 us
  waiting for transfers between devices  527 us (54%)
  matrix products  222 us (23%)
  local copies, waits for them, and re-layouts  98.2 us (10%)
  blocking collectives  68.6 us (7%)
  other arithmetic  27.7 us (3%)
  between operations  16.5 us (2%)
    unnamed x16, waiting for transfers between devices  145 us
    unnamed x81, local copies, waits for them, and re-layouts  80.3 us
    reduce_scatter x1, waiting for transfers between devices, on_device(): lax.psum_scatter(grad_inner_weight.astype(jnp.bfloat16), 'seq', scatter_d...  60.1 us
    reduce_scatter x1, waiting for transfers between devices, on_device(): lax.psum_scatter(grad_outer_weight.astype(jnp.bfloat16), 'seq', scatter_d...  60 us
    all_gather x1, waiting for transfers between devices, on_device(): key_part = lax.all_gather(keys_low, 'ctx', axis=1, tiled=True)  58.8 us
    psum x1, waiting for transfers between devices, on_device(): lax.psum(owned[0].astype(jnp.bfloat16), 'ctx').astype(jnp.float32)  47.9 us
    all_gather x1, waiting for transfers between devices, on_device(): lax.all_gather(outer_weight, 'seq', axis=0, tiled=True)  39 us
    all_gather x1, waiting for transfers between devices, on_device(): value_part = lax.all_gather(values_low, 'ctx', axis=1, tiled=True)  36.3 us
  transfers between devices with their start and end apart: 13, of which 12 were waited for; matrix products, arithmetic and copies ran while one was open for 17% of the time, Pallas kernels for 0%

commit v1 on v0

--- a/solution.py
+++ b/solution.py
@@ -7,6 +7,18 @@
 HEADS = 12
 HEAD_DIM = 64
 norm_epsilon = 1e-12
+
+
+def collect(x, axis, dim):
+    ways, here, step = (lax.axis_size(axis), lax.axis_index(axis), x.shape[dim])
+    line, have = (x, 1)
+    while have < ways:
+        line = jnp.concatenate(
+            [line, lax.ppermute(line, axis, [(d, (d - have) % ways) for d in range(ways)])],
+            axis=dim,
+        )
+        have = 2 * have
+    return jnp.roll(line, here * step, axis=dim)
 
 
 def norm_forward(matrix, gain, shift):
@@ -85,7 +97,7 @@
     row_count = groups * positions
     scaling = HEAD_DIM ** (-0.5)
     gathered = (
-        lax.all_gather(qkv_weight, "seq", axis=0, tiled=True),
+        collect(qkv_weight, "seq", 0),
         lax.all_gather(query_bias, "seq", axis=0, tiled=True),
         lax.all_gather(value_bias, "seq", axis=0, tiled=True),
         lax.all_gather(out_weight, "seq", axis=0, tiled=True),

time: 970 us -> 1030 us (1.062)
  waiting for transfers between devices: 527 us -> 580 us
    psum x1, waiting for transfers between devices: 47.9 us -> 88.6 us  [on_device(): lax.psum(owned[0].astype(jnp.bfloat16), 'ctx').astype(jnp.float32)]
    ppermute x0 -> x2, waiting for transfers between devices: none -> 30.1 us  [collect(): lax.ppermute(line, axis, [(d, (d - have) % ways) for d in range(ways)])]
    all_gather x1, waiting for transfers between devices: 26.3 us -> 8.85 us  [on_device(): lax.all_gather(qkv_weight, 'seq', axis=0, tiled=True)]
    unnamed x81 -> x108, local copies, waits for them, and re-layouts: 80.3 us -> 82.4 us
  transfers between devices with their start and end apart: 13 -> 15, of which waited for: 12 -> 14; matrix products, arithmetic and copies ran while one was open for 17% -> 16% of each run, Pallas kernels for 0% -> 0%
where the time goes in v1:
time: 1030 us; the launch traced here: 1020 us
  waiting for transfers between devices  580 us (56%)
  matrix products  220 us (21%)
  local copies, waits for them, and re-layouts  100 us (10%)
  blocking collectives  68.5 us (7%)
  other arithmetic  31.5 us (3%)
  between operations  16.7 us (2%)
    unnamed x16, waiting for transfers between devices  145 us
    psum x1, waiting for transfers between devices, on_device(): lax.psum(owned[0].astype(jnp.bfloat16), 'ctx').astype(jnp.float32)  88.6 us
    unnamed x108, local copies, waits for them, and re-layouts  82.4 us
    reduce_scatter x1, waiting for transfers between devices, on_device(): lax.psum_scatter(grad_inner_weight.astype(jnp.bfloat16), 'seq', scatter_d...  60.1 us
    reduce_scatter x1, waiting for transfers between devices, on_device(): lax.psum_scatter(grad_outer_weight.astype(jnp.bfloat16), 'seq', scatter_d...  60 us
    all_gather x1, waiting for transfers between devices, on_device(): key_part = lax.all_gather(keys_low, 'ctx', axis=1, tiled=True)  58.9 us
    all_gather x1, waiting for transfers between devices, on_device(): lax.all_gather(outer_weight, 'seq', axis=0, tiled=True)  38.9 us
    all_gather x1, waiting for transfers between devices, on_device(): value_part = lax.all_gather(values_low, 'ctx', axis=1, tiled=True)  37 us
  transfers between devices with their start and end apart: 15, of which 14 were waited for; matrix products, arithmetic and copies ran while one was open for 16% of the time, Pallas kernels for 0%

profile of v1, /device:TPU:0, one launch (start us, length us, event | category | flops | bytes accessed | tf_op | source)
XLA Modules:
  0.0 1024.7 jit_solution(10444486896741572741)
XLA Ops:
  11.2 19.2 %collective-permute-done = bf16[192,2304]{1,0:T(8,128)(2,1)S(1)} collective-permute-done((bf16[192,2304]{1,0:T(8,128)(2,1)}, bf16[192,2304]{1,0:T(8,128)(2,1)S(1)}, u32[]{:S(2)}, u32[]{:S(2)}) %collective-permute-start) | collective-permute-done | bytes 884768 | tf_op jit(solution)/shard_map/ppermute | solution.py:17
  43.0 17.6 %all-reduce.20 = (bf16[768]{0:T(1024)(128)(2,1)}, bf16[768]{0:T(1024)(128)(2,1)}, bf16[768]{0:T(1024)(128)(2,1)}, bf16[768]{0:T(1024)(128)(2,1)}, bf16[768]{0:T(...) all-reduce(bf16[768]{0:T(1024)(128)(2,1)S(1)} %dynamic-update-slice, ...), channel_id=1, replica_groups=mesh['seq'=4,'ctx'=8] {'seq'}, use_global_device_ids=true, to_apply=%add | all-reduce | flops 5376 | bytes 21504
  62.1 10.9 %collective-permute-done.1 = bf16[384,2304]{1,0:T(8,128)(2,1)S(1)} collective-permute-done((bf16[384,2304]{1,0:T(8,128)(2,1)}, bf16[384,2304]{1,0:T(8,128)(2,1)S(1)}, u32[]{:S(2)}, u32[]{:S(2)}) %collective-permute-start.1) | collective-permute-done | bytes 1769504 | tf_op jit(solution)/shard_map/ppermute | solution.py:17
  84.5 12.1 %all_gather.58 = bf16[4,1024]{1,0:T(4,128)(2,1)S(1)} all-gather(bf16[4,128]{1,0:T(4,128)(2,1)S(1)} %convert_element_type.236), channel_id=1, replica_groups=mesh['seq'=4,'ctx'=8] {'ctx'}, dimensions={1}, use_global_device_ids=true | all-gather | bytes 9216 | tf_op jit(solution)/shard_map/all_gather | solution.py:155
  96.6 8.9 all-gather
  109.8 37.0 %all-gather.10.cloned.1.call-done = bf16[4,1024,768]{1,2,0:T(8,128)(2,1)} async-done(((bf16[4,128,768]{1,2,0:T(8,128)(2,1)}), bf16[4,1024,768]{1,2,0:T(8,128)(2,1)}) %all-gather.10.cloned.1.call-update) | async-done | bytes 6291472 | tf_op jit(solution)/shard_map/all_gather | solution.py:154
  146.9 6.7 copy.57
  153.6 58.9 %all-gather.8.cloned.1.call-done = bf16[4,1024,768]{1,2,0:T(8,128)(2,1)} async-done(((bf16[4,128,768]{1,2,0:T(8,128)(2,1)}), bf16[4,1024,768]{1,2,0:T(8,128)(2,1)}) %all-gather.8.cloned.1.call-update) | async-done | bytes 6291472 | tf_op jit(solution)/shard_map/all_gather | solution.py:153
  212.4 6.7 copy.56
  219.1 51.8 %while.30 = (s32[]{:T(128)}, f32[12,4,128]{2,1,0:T(4,128)S(1)}, f32[12,4,128]{2,1,0:T(4,128)S(1)}, f32[12,4,128,64]{2,1,3,0:T(4,128)S(1)}, bf16[12,4,128,64]{2,3...) while((s32[]{:T(128)}, f32[12,4,128]{2,1,0:T(4,128)S(1)}, ...), condition=%wide.region_3.4_spmd.clone, body=%wide.region_0.3_spmd.clone.sunk | while | flops 142641664 | bytes 7852653 | solution.py:177
  275.0 24.0 %all-gather.14.cloned.1.call-done = bf16[768,3072]{1,0:T(8,128)(2,1)} async-done(((bf16[192,3072]{1,0:T(8,128)(2,1)}), bf16[768,3072]{1,0:T(8,128)(2,1)}) %all-gather.14.cloned.1.call-update) | async-done | bytes 4718608 | tf_op jit(solution)/shard_map/all_gather | solution.py:107
  299.0 19.8 %multiply_convert_fusion.1 = (bf16[512,3072]{1,0:T(8,128)(2,1)}, f32[512,3072]{1,0:T(8,128)}, f32[512,3072]{1,0:T(8,128)}) fusion(f32[3072]{0:T(1024)S(1)} %bitcast.238, bf16[768,3072]{1,0:T(8,128)(2,1)} %all-gather.14.cloned.1.call-done, f32[512,768]{1,0:T(8,128)S(1)} %get-tuple-element.358, f32[768]{0:T(1024)S(1)} %convert_element_type.244, ...), kind=kOutput, calls=%fused_computation.66 | convolution fusion | flops 2521694208 | bytes 22042624 | tf_op jit(solution)/shard_map/dot_general | solution.py:195
  318.9 38.9 %all-gather.16.cloned.1.call-done = bf16[3072,768]{1,0:T(8,128)(2,1)} async-done(((bf16[768,768]{1,0:T(8,128)(2,1)}), bf16[3072,768]{1,0:T(8,128)(2,1)}) %all-gather.16.cloned.1.call-update) | async-done | bytes 4718608 | tf_op jit(solution)/shard_map/all_gather | solution.py:109
  357.8 6.5 fusion.86
  367.4 9.2 fusion.87
  389.1 103.7 %while.31 = (s32[]{:T(128)}, bf16[12,4,128,64]{2,3,1,0:T(8,128)(2,1)}, bf16[12,4,1024,64]{2,3,0,1:T(8,128)(2,1)}, bf16[12,4,1024,64]{2,3,0,1:T(8,128)(2,1)}, bf1...) while((s32[]{:T(128)}, ...), condition=%wide.region_14.15_spmd.clone, body=%wide.region_13.14_spmd.clone.sunk | while | flops 340033536 | bytes 13657221 | solution.py:256
  492.8 10.8 %copy.70 = bf16[4,1024,768]{2,0,1:T(4,128)(2,1)} copy(bf16[4,1024,768]{1,2,0:T(8,128)(2,1)} %bitcast.220) | data formatting | bytes 12582912
  503.6 6.9 copy.100
  510.6 11.0 %copy.72 = bf16[4,1024,768]{2,0,1:T(4,128)(2,1)} copy(bf16[4,1024,768]{1,2,0:T(8,128)(2,1)} %bitcast.221) | data formatting | bytes 12582912
  521.6 7.0 copy.102
  531.4 49.1 %reduce-scatter.19.cloned.1.call-done = bf16[128,3072]{1,0:T(8,128)(2,1)} async-done(((bf16[1024,3072]{1,0:T(8,128)(2,1)}), bf16[128,3072]{1,0:T(8,128)(2,1)}) %reduce-scatter.19.cloned.1.call-update) | async-done | bytes 786448
  583.8 67.2 %reduce-scatter.21.cloned.1.call-done = bf16[128,3072]{1,0:T(8,128)(2,1)} async-done(((bf16[1024,3072]{1,0:T(8,128)(2,1)}), bf16[128,3072]{1,0:T(8,128)(2,1)}) %reduce-scatter.21.cloned.1.call-update) | async-done | bytes 786448
  673.7 7.7 convolution_convert_fusion
  681.5 7.6 convolution_convert_fusion.1
  689.7 25.9 %reduce-scatter.23.cloned.1.call-done = bf16[192,2304]{1,0:T(8,128)(2,1)} async-done(((bf16[768,2304]{1,0:T(8,128)(2,1)}), bf16[192,2304]{1,0:T(8,128)(2,1)}) %reduce-scatter.23.cloned.1.call-update) | async-done | bytes 884752
  718.0 29.2 %reduce-scatter.13.cloned.1.call-done = bf16[192,768]{1,0:T(8,128)(2,1)} async-done(((bf16[768,768]{1,0:T(8,128)(2,1)}), bf16[192,768]{1,0:T(8,128)(2,1)}) %reduce-scatter.13.cloned.1.call-update) | async-done | bytes 294928 | tf_op jit(solution)/shard_map/reduce_scatter | solution.py:298
  747.1 60.0 %reduce-scatter.17.cloned.1.call-done = bf16[768,768]{1,0:T(8,128)(2,1)} async-done(((bf16[3072,768]{1,0:T(8,128)(2,1)}), bf16[768,768]{1,0:T(8,128)(2,1)}) %reduce-scatter.17.cloned.1.call-update) | async-done | bytes 1179664 | tf_op jit(solution)/shard_map/reduce_scatter | solution.py:316
  807.1 60.1 %reduce-scatter.15.cloned.1.call-done = bf16[192,3072]{1,0:T(8,128)(2,1)} async-done(((bf16[768,3072]{1,0:T(8,128)(2,1)}), bf16[192,3072]{1,0:T(8,128)(2,1)}) %reduce-scatter.15.cloned.1.call-update) | async-done | bytes 1179664 | tf_op jit(solution)/shard_map/reduce_scatter | solution.py:310
  870.8 16.0 %all-reduce.19 = (bf16[768]{0:T(1024)(128)(2,1)S(1)}, bf16[768]{0:T(1024)(128)(2,1)S(1)}, bf16[768]{0:T(1024)(128)(2,1)S(1)}, bf16[768]{0:T(1024)(128)(2,1)S(1)}...) all-reduce(bf16[768]{0:T(1024)(128)(2,1)S(1)} %dynamic-update-slice, ...), channel_id=1, replica_groups=mesh['seq'=4,'ctx'=8] {'seq'}, use_global_device_ids=true, to_apply=%add.7 | all-reduce | flops 9984 | bytes 39936
  887.5 13.9 %all-reduce.17 = (bf16[192]{0:T(256)(128)(2,1)S(1)}, bf16[192]{0:T(256)(128)(2,1)S(1)}, bf16[192]{0:T(256)(128)(2,1)S(1)}, bf16[192]{0:T(256)(128)(2,1)S(1)}, bf...) all-reduce(bf16[192]{0:T(256)(128)(2,1)S(1)} %dynamic-slice.9, ...), channel_id=1, replica_groups=mesh['seq'=4,'ctx'=8] {'ctx'}, use_global_device_ids=true, to_apply=%region_21.22 | all-reduce | flops 2304 | bytes 9216 | tf_op jit(solution)/shard_map/psum | solution.py:331
  907.6 8.8 all-gather.18.cloned.1.call-done
  922.4 88.6 %all-reduce.23.cloned.1.call-done = (bf16[192,2304]{0,1:T(8,128)(2,1)}, bf16[192,768]{1,0:T(8,128)(2,1)}, bf16[192,3072]{1,0:T(8,128)(2,1)}, bf16[768,768]{1,0:T(8,128)(2,1)}) async-done(((bf16[192,2304]{0,1:T(8,128)(2,1)}, bf16[192,768]{1,0:T(8,128)(2,1)}, bf16[192,3072]{1,0:T(8,128)(2,1)}, bf16[768,768]{1,0:T(8,128)(2,1)}), (bf16[192,2304]{0,1:T(8,128)(2,1)}, bf16[192,768]{1,0:T(8,128)(2,1)}, ...) | async-done | bytes 3538960 | tf_op jit(solution)/shard_map/psum | solution.py:330
  (358 shorter events, 260.9 us)
Async XLA Ops:
  7.2 27.2 %copy-start.18 = (u32[32]{0:T(128)S(1)}, u32[32]{0:T(128)}, u32[]{:S(2)}) copy-start(u32[32]{0:T(128)} %constant.166) | copy-start | bytes 388
  7.2 54.8 %copy-start = (bf16[192,2304]{1,0:T(8,128)(2,1)S(1)}, bf16[192,2304]{1,0:T(8,128)(2,1)}, u32[]{:S(2)}) copy-start(bf16[192,2304]{1,0:T(8,128)(2,1)} %param.23) | copy-start | bytes 2654212
  7.2 28.4 %copy-start.25 = (bf16[192]{0:T(256)(128)(2,1)S(1)}, bf16[192]{0:T(256)(128)(2,1)}, u32[]{:S(2)}) copy-start(bf16[192]{0:T(256)(128)(2,1)} %param.24) | copy-start | bytes 1156
  7.2 28.7 %copy-start.26 = (bf16[192]{0:T(256)(128)(2,1)S(1)}, bf16[192]{0:T(256)(128)(2,1)}, u32[]{:S(2)}) copy-start(bf16[192]{0:T(256)(128)(2,1)} %param.25) | copy-start | bytes 1156
  7.2 28.9 %copy-start.27 = (bf16[192]{0:T(256)(128)(2,1)S(1)}, bf16[192]{0:T(256)(128)(2,1)}, u32[]{:S(2)}) copy-start(bf16[192]{0:T(256)(128)(2,1)} %param.27) | copy-start | bytes 1156
  7.2 139.6 %all-gather.10.cloned.1.call-start = ((), (), s32[]{:S(2)}) async-start(), calls=%async_computation.7 | async-start | bytes 7077888 | tf_op jit(solution)/shard_map/all_gather | solution.py:154
  7.3 23.2 %collective-permute-start = (bf16[192,2304]{1,0:T(8,128)(2,1)}, bf16[192,2304]{1,0:T(8,128)(2,1)S(1)}, u32[]{:S(2)}, u32[]{:S(2)}) collective-permute-start(bf16[192,2304]{1,0:T(8,128)(2,1)} %param.23), channel_id=1, source_target_pairs={{0,24},{8,0},{16,8},{24,16},{1,25},{9,1},{17,9},{25,17},{2,26},{10... | collective-permute-start | bytes 2654216 | tf_op jit(solution)/shard_map/ppermute | solution.py:17
  32.9 40.0 %collective-permute-start.1 = (bf16[384,2304]{1,0:T(8,128)(2,1)}, bf16[384,2304]{1,0:T(8,128)(2,1)S(1)}, u32[]{:S(2)}, u32[]{:S(2)}) collective-permute-start(bf16[384,2304]{1,0:T(8,128)(2,1)} %pad_maximum_fusion), channel_id=1, source_target_pairs={{0,16},{8,24},{16,0},{24,8},{1,17},{9,25},{17,1},{25,9},{2,18},{10... | collective-permute-start | bytes 5308424 | tf_op jit(solution)/shard_map/ppermute | solution.py:17
  79.6 132.8 %all-gather.8.cloned.1.call-start = ((), (), s32[]{:S(2)}) async-start(), calls=%async_computation.6 | async-start | bytes 7077888 | tf_op jit(solution)/shard_map/all_gather | solution.py:153
  81.2 15.4 %copy-start.17 = (bf16[768]{0:T(1024)(128)(2,1)S(1)}, bf16[768]{0:T(1024)(128)(2,1)}, u32[]{:S(2)}) copy-start(bf16[768]{0:T(1024)(128)(2,1)} %get-tuple-element.334) | copy-start | bytes 4612
  81.2 15.3 %copy-start.16 = (bf16[768]{0:T(1024)(128)(2,1)S(1)}, bf16[768]{0:T(1024)(128)(2,1)}, u32[]{:S(2)}) copy-start(bf16[768]{0:T(1024)(128)(2,1)} %get-tuple-element.336) | copy-start | bytes 4612
  81.2 15.3 %copy-start.15 = (bf16[768]{0:T(1024)(128)(2,1)S(1)}, bf16[768]{0:T(1024)(128)(2,1)}, u32[]{:S(2)}) copy-start(bf16[768]{0:T(1024)(128)(2,1)} %get-tuple-element.335) | copy-start | bytes 4612
  81.2 15.4 %copy-start.20 = (bf16[768]{0:T(1024)(128)(2,1)S(1)}, bf16[768]{0:T(1024)(128)(2,1)}, u32[]{:S(2)}) copy-start(bf16[768]{0:T(1024)(128)(2,1)} %param.31) | copy-start | bytes 4612
  81.2 24.3 %copy-start.14 = (bf16[768]{0:T(1024)(128)(2,1)S(1)}, bf16[768]{0:T(1024)(128)(2,1)}, u32[]{:S(2)}) copy-start(bf16[768]{0:T(1024)(128)(2,1)} %get-tuple-element.337) | copy-start | bytes 4612
  81.2 24.3 %copy-start.13 = (bf16[768]{0:T(1024)(128)(2,1)S(1)}, bf16[768]{0:T(1024)(128)(2,1)}, u32[]{:S(2)}) copy-start(bf16[768]{0:T(1024)(128)(2,1)} %get-tuple-element.338) | copy-start | bytes 4612
  81.3 24.3 %copy-start.1 = (bf16[4,128,768]{2,1,0:T(8,128)(2,1)S(1)}, bf16[4,128,768]{2,1,0:T(8,128)(2,1)}, u32[]{:S(2)}) copy-start(bf16[4,128,768]{2,1,0:T(8,128)(2,1)} %param.21) | copy-start | bytes 2359300
  82.4 188.8 %all-gather.12.cloned.1.call-start = ((), (), s32[]{:S(2)}) async-start(), calls=%async_computation.8 | async-start | bytes 1474560 | tf_op jit(solution)/shard_map/all_gather | solution.py:103
  83.2 215.9 %all-gather.14.cloned.1.call-start = ((), (), s32[]{:S(2)}) async-start(), calls=%async_computation.9 | async-start | bytes 5898240 | tf_op jit(solution)/shard_map/all_gather | solution.py:107
  83.8 274.1 %all-gather.16.cloned.1.call-start = ((), (), s32[]{:S(2)}) async-start(), calls=%async_computation.10 | async-start | bytes 5898240 | tf_op jit(solution)/shard_map/all_gather | solution.py:109
  84.3 496.1 %reduce-scatter.19.cloned.1.call-start = ((), (), s32[]{:S(2)}) async-start(), calls=%async_computation.15 | async-start | bytes 7077888
  274.7 44.2 %copy-start.4 = (f32[512,768]{1,0:T(8,128)}, f32[512,768]{1,0:T(8,128)S(1)}, u32[]{:S(2)}) copy-start(f32[512,768]{1,0:T(8,128)S(1)} %get-tuple-element.358) | copy-start | bytes 4718596
  365.3 11.3 %slice-start = ((s8[4718592]{0:T(1024)(128)(4,1)}), s8[4194304]{0:T(1024)(128)(4,1)S(1)}, s32[]{:S(2)}) async-start(s8[4718592]{0:T(1024)(128)(4,1)} %bitcast.240), calls=%async_computation.19 | async-start | bytes 8388608
  365.9 10.7 %copy-start.9 = (f32[512,768]{1,0:T(8,128)}, f32[512,768]{1,0:T(8,128)S(1)}, u32[]{:S(2)}) copy-start(f32[512,768]{1,0:T(8,128)S(1)} %get-tuple-element.340) | copy-start | bytes 4718596
  510.5 140.5 %reduce-scatter.21.cloned.1.call-start = ((), (), s32[]{:S(2)}) async-start(), calls=%async_computation.16 | async-start | bytes 7077888
  528.6 187.0 %reduce-scatter.23.cloned.1.call-start = ((), (), s32[]{:S(2)}) async-start(), calls=%async_computation.17 | async-start | bytes 4423680
  669.9 77.2 %reduce-scatter.13.cloned.1.call-start = ((), (), s32[]{:S(2)}) async-start(), calls=%async_computation.12 | async-start | bytes 1474560 | tf_op jit(solution)/shard_map/reduce_scatter | solution.py:298
  673.5 133.7 %reduce-scatter.17.cloned.1.call-start = ((), (), s32[]{:S(2)}) async-start(), calls=%async_computation.14 | async-start | bytes 5898240 | tf_op jit(solution)/shard_map/reduce_scatter | solution.py:316
  681.4 185.8 %reduce-scatter.15.cloned.1.call-start = ((), (), s32[]{:S(2)}) async-start(), calls=%async_computation.13 | async-start | bytes 5898240 | tf_op jit(solution)/shard_map/reduce_scatter | solution.py:310
  689.1 227.4 %all-gather.18.cloned.1.call-start = ((), (), s32[]{:S(2)}) async-start(), calls=%async_computation.11 | async-start | bytes 4423680 | tf_op jit(solution)/shard_map/all_gather | solution.py:201
  689.7 321.3 %all-reduce.23.cloned.1.call-start = ((), (), s32[]{:S(2)}) async-start(), calls=%async_computation.18 | async-start | bytes 7667712 | tf_op jit(solution)/shard_map/psum | solution.py:330
  718.0 150.8 %copy-start.28 = (bf16[192]{0:T(256)(128)(2,1)S(1)}, bf16[192]{0:T(256)(128)(2,1)}, u32[]{:S(2)}) copy-start(bf16[192]{0:T(256)(128)(2,1)} %param.35) | copy-start | bytes 1156
  870.8 45.7 %copy-start.3 = (f32[512,768]{1,0:T(8,128)S(1)}, f32[512,768]{1,0:T(8,128)}, u32[]{:S(2)}) copy-start(f32[512,768]{1,0:T(8,128)} %copy-done.2) | copy-start | bytes 4718596
  (14 other events, 45.7 us)
Sparse Core Ops, SparseCore 0:
  79.8 67.0 all-gather.9
  149.0 63.3 all-gather.7
  214.3 25.9 all-gather.11
  241.9 57.0 all-gather.13
  300.7 57.0 all-gather.15
  510.7 69.7 reduce-scatter.18
  582.8 68.1 reduce-scatter.20
  670.0 45.5 reduce-scatter.22
  718.6 28.5 reduce-scatter.12
  750.0 57.0 reduce-scatter.16
  810.1 57.0 reduce-scatter.14
  868.9 47.4 all-gather.17
  919.7 91.2 all-reduce.22
